TPU v7x, 32 devices: a whole 2x2x4 slice. The times are simulated.
32 devices in a mesh: row: 8 (over y, x, core), col: 4 (over z).
Axes of the slice: x: 2, y: 2, z: 4, core: 2. Of those that a mesh axis runs over, the one named last changes fastest.
Arguments:
- pooled: bfloat16 [4096, 1152], P(('row', 'col')), may hold values from -6 to 6
- text_embed: bfloat16 [4096, 1152], P(('row', 'col')), may hold values from -0.29882812 to 0.29882812
- head_weight: bfloat16 [1152, 1152], replicated, may hold values from -0.1875 to 0.1875
- logit_scale: float32 [4], replicated, may hold values from 1 to 4
- logit_bias: float32 [4], replicated, may hold values from -2 to 0
- partner: int32 [32, 128], P(('row', 'col')), may hold values from 0 to 127, each once within a row
Outputs:
- text_grad: float32 [4096, 1152], P(('row', 'col'))
- head_grad: float32 [1152, 1152], P('row', 'col')
Inputs may be any that keep to these rules, and one draw needn't show every extreme that they name: Each row of partner is a permutation of the indices within a block.
All inputs are finite; a program needn't handle non-finite values.
Results may differ from a plain program's by a relative error of at most 0.004.
Values may be sent and summed in bfloat16 or wider, within the bound.
A program may use at most 64 MiB of HBM per device.

v0:
```python
import functools
import math

import jax
import jax.numpy as jnp
from jax import lax
from jax.experimental import pallas as pl
from jax.experimental.pallas import tpu as pltpu
from jax.sharding import PartitionSpec as P

LANES = 128
MESH = pl.DeviceIdType.MESH


def shifted(value, axis, by):
    count = lax.axis_size(axis)
    return lax.ppermute(value, axis, [(i, (i + by) % count) for i in range(count)])


def segment_weights(image_part, text_part, positive, logit_scale, logit_bias, factor):
    model_width = image_part.shape[1]
    bounds = [0, model_width // 8, model_width // 4, model_width // 2, model_width]
    running = jnp.zeros((image_part.shape[0], text_part.shape[0]), jnp.float32)
    level_grads = []
    for prefix in range(4):
        low_end = bounds[prefix]
        high_end = bounds[prefix + 1]
        running = running + jnp.dot(
            image_part[:, low_end:high_end],
            text_part[:, low_end:high_end].T,
            preferred_element_type=jnp.float32,
        )
        logits = logit_scale[prefix] * running + logit_bias[prefix]
        level_grads.append((jax.nn.sigmoid(logits) - positive) * factor)
    weights = []
    carried = jnp.zeros_like(running)
    for prefix in range(3, -1, -1):
        carried = carried + logit_scale[prefix] * level_grads[prefix]
        weights.insert(0, carried.astype(jnp.bfloat16))
    return (weights, bounds)


def image_side(weights, bounds, text_part):
    pieces = []
    for prefix in range(4):
        pieces.append(
            jnp.dot(
                weights[prefix],
                text_part[:, bounds[prefix] : bounds[prefix + 1]],
                preferred_element_type=jnp.float32,
            )
        )
    return jnp.concatenate(pieces, 1)


def text_side(weights, bounds, image_part):
    pieces = []
    for prefix in range(4):
        pieces.append(
            jnp.dot(
                weights[prefix].T,
                image_part[:, bounds[prefix] : bounds[prefix + 1]],
                preferred_element_type=jnp.float32,
            )
        )
    return jnp.concatenate(pieces, 1)


def body(pooled, text_embed, head_weight, logit_scale, logit_bias, partner):
    block_rows = pooled.shape[0]
    factor = 1.0 / math.sqrt(block_rows * lax.axis_size("row") * lax.axis_size("col"))
    embedding = jnp.dot(pooled, head_weight, preferred_element_type=jnp.float32).astype(
        jnp.bfloat16
    )
    local_ids = jnp.arange(block_rows, dtype=jnp.int32)
    positive = (partner[0][:, None] == local_ids[None, :]).astype(jnp.float32)
    empty = jnp.zeros((block_rows, block_rows), jnp.float32)
    weights, bounds = segment_weights(
        embedding, text_embed, positive, logit_scale, logit_bias, factor
    )
    own_image = image_side(weights, bounds, text_embed)
    own_text = text_side(weights, bounds, embedding)
    behind = shifted(text_embed, "row", 1)
    weights, bounds = segment_weights(embedding, behind, empty, logit_scale, logit_bias, factor)
    cross_image = image_side(weights, bounds, behind)
    cross_text = text_side(weights, bounds, embedding)
    returned = shifted(cross_text.astype(jnp.bfloat16), "row", -1).astype(cross_text.dtype)
    text_grad = own_text + returned
    image_grad = own_image + cross_image
    column_block = lax.all_to_all(
        image_grad.astype(jnp.bfloat16), "col", split_axis=1, concat_axis=0, tiled=True
    ).astype(image_grad.dtype)
    group_rows = lax.all_gather(pooled, "col", axis=0, tiled=True)
    block_term = jnp.dot(
        group_rows.astype(jnp.float32).T, column_block, precision=lax.Precision.HIGHEST
    )
    head_grad = lax.psum_scatter(block_term, "row", scatter_dimension=0, tiled=True)
    return (text_grad, head_grad)


def dot_nt(left, right):
    return lax.dot_general(
        left, right, (((1,), (1,)), ((), ())), preferred_element_type=jnp.float32
    )


def dot_nn(left, right):
    return jnp.dot(left, right, preferred_element_type=jnp.float32)


def aligned(low_end, high_end):
    return low_end // LANES * LANES, -(-high_end // LANES) * LANES


def weights_of(score_of, positive, scale_ref, bias_ref, factor):
    running = None
    level_grads = []
    for prefix in range(4):
        part = score_of(prefix)
        running = part if running is None else running + part
        gate = jax.nn.sigmoid(scale_ref[prefix] * running + bias_ref[prefix])
        if positive is not None:
            gate = gate - positive
        level_grads.append(gate * factor)
    weights = [None] * 4
    carried = None
    for prefix in range(3, -1, -1):
        term = scale_ref[prefix] * level_grads[prefix]
        carried = term if carried is None else carried + term
        weights[prefix] = carried.astype(jnp.bfloat16)
    return weights


def by_tile(piece_of, bounds, store):
    pieces = []
    for q in range(4):
        start, stop = aligned(bounds[q], bounds[q + 1])
        pieces.append((start, stop, piece_of(q, start, stop)))
    for tile in range(bounds[4] // LANES):
        base = tile * LANES
        value = None
        for q in range(4):
            start, stop, piece = pieces[q]
            if start <= base < stop:
                here = piece[:, base - start : base - start + LANES]
                if value is None:
                    value = here
                else:
                    lane = lax.broadcasted_iota(jnp.int32, here.shape, 1)
                    value = jnp.where(lane < bounds[q] - base, value, here)
        store(base, value)


def kernel(
    n_row,
    n_col,
    factor,
    chunks,
    ready,
    window,
    tail_rows,
    pooled_ref,
    text_ref,
    weight_hbm,
    scale_ref,
    bias_ref,
    partner_ref,
    text_grad_ref,
    head_grad_ref,
    weight_ref,
    weight_sem,
    image_own,
    cross_text,
    text_back,
    text_behind,
    pooled_t,
    pooled_cols,
    embed,
    masked,
    image,
    total,
    sent,
    landed,
    near_send,
    near_recv,
    pool_send,
    pool_recv,
    image_send,
    image_recv,
    out_send,
    out_recv,
):
    rows, width = pooled_ref.shape
    chips = n_row // 2
    head_rows = width // n_row
    head_cols = width // n_col
    bounds = [0, width // 8, width // 4, width // 2, width]
    row = lax.axis_index("row")
    col = lax.axis_index("col")
    chip = row // 2
    core = row % 2

    side = chip % 2
    level = chip // 2

    def peer(k, e):
        there = chip + (k % 2) * (1 - 2 * side) + (k // 2) * (2 - 4 * level)
        return there * 2 + (core if e == 0 else 1 - core)

    weight_copy = pltpu.make_async_copy(weight_hbm, weight_ref, weight_sem)
    weight_copy.start()

    barrier = pltpu.get_barrier_semaphore()
    for d in range(1, n_row):
        pl.semaphore_signal(
            barrier, inc=1, device_id=((row + d) % n_row, col), device_id_type=MESH
        )
    for d in range(1, n_col):
        pl.semaphore_signal(
            barrier, inc=1, device_id=(row, (col + d) % n_col), device_id_type=MESH
        )

    def remote(src, dst, send, recv, device):
        return pltpu.make_async_remote_copy(
            src_ref=src,
            dst_ref=dst,
            send_sem=send,
            recv_sem=recv,
            device_id=device,
            device_id_type=MESH,
        )

    behind_copy = remote(
        text_ref, text_behind, near_send.at[0], near_recv.at[0], ((row + 1) % n_row, col)
    )
    back_copy = remote(
        cross_text,
        text_back,
        near_send.at[1],
        near_recv.at[1],
        ((row + n_row - 1) % n_row, col),
    )
    pl.semaphore_wait(barrier, n_row + n_col - 2)
    behind_copy.start()

    for tile in range(width // LANES):
        lanes = pl.ds(tile * LANES, LANES)
        pooled_t[lanes, :] = pooled_ref[:, lanes].T
    pool_copies = []
    for k in range(chips):
        for e in range(2):
            slot = 2 * k + e
            if slot == 0:
                continue
            target = peer(k, e)
            copy = remote(
                pooled_t.at[pl.ds(pl.multiple_of(target * head_rows, 16), head_rows), :],
                pooled_cols.at[:, pl.ds(slot * rows, rows)],
                pool_send.at[slot],
                pool_recv.at[slot],
                (target, col),
            )
            pool_copies.append(copy)
    pooled_cols[:, pl.ds(0, rows)] = pooled_t[
        pl.ds(pl.multiple_of(row * head_rows, 16), head_rows), :
    ]

    def fill_embed(source):
        at = 0
        for q in range(4):
            start, stop = aligned(bounds[q], bounds[q + 1])
            at += stop - start
        step = 3 * LANES if width % (3 * LANES) == 0 else LANES
        for base in range(0, width, step):
            part = dot_nn(source[...], weight_ref[:, pl.ds(base, step)])
            embed[:, pl.ds(base, step)] = part.astype(jnp.bfloat16)
        at = 0
        for q in range(4):
            start, stop = aligned(bounds[q], bounds[q + 1])
            part = embed[:, pl.ds(start, stop - start)].astype(jnp.float32)
            lane = lax.broadcasted_iota(jnp.int32, part.shape, 1) + start
            keep = (lane >= bounds[q]) & (lane < bounds[q + 1])
            masked[:, pl.ds(at, stop - start)] = jnp.where(keep, part, 0.0).astype(
                jnp.bfloat16
            )
            at += stop - start

    def masked_part(q):
        at = 0
        for before in range(q):
            start, stop = aligned(bounds[before], bounds[before + 1])
            at += stop - start
        start, stop = aligned(bounds[q], bounds[q + 1])
        return masked[:, pl.ds(at, stop - start)]

    def text_part(ref, q):
        start, stop = aligned(bounds[q], bounds[q + 1])
        return ref[:, pl.ds(start, stop - start)]

    for copy in pool_copies:
        copy.start()
    weight_copy.wait()
    fill_embed(pooled_ref)
    text_id = lax.broadcasted_iota(jnp.int32, (rows, rows), 0)
    positive = (text_id == partner_ref[...]).astype(jnp.float32).T
    own = weights_of(
        lambda q: dot_nt(masked_part(q), text_part(text_ref, q)),
        positive,
        scale_ref,
        bias_ref,
        factor,
    )

    def own_image_piece(q, start, stop):
        return dot_nn(own[q], text_ref[:, pl.ds(start, stop - start)])

    def keep_image(base, value):
        image_own[:, pl.ds(base, LANES)] = value

    by_tile(own_image_piece, bounds, keep_image)

    def own_text_piece(q, start, stop):
        return dot_nn(own[q].T, embed[:, pl.ds(start, stop - start)])

    def store_text(base, value):
        text_grad_ref[:, pl.ds(base, LANES)] = value

    by_tile(own_text_piece, bounds, store_text)

    behind_copy.wait_recv()
    cross = weights_of(
        lambda q: dot_nt(masked_part(q), text_part(text_behind, q)),
        None,
        scale_ref,
        bias_ref,
        factor,
    )

    def image_piece(q, start, stop):
        lanes = pl.ds(start, stop - start)
        return dot_nn(cross[q], text_behind[:, lanes])

    def store_image(base, value):
        lanes = pl.ds(base, LANES)
        image[pl.ds(0, rows), lanes] = (image_own[:, lanes] + value).astype(jnp.bfloat16)

    by_tile(image_piece, bounds, store_image)

    chunk = width // chunks
    half = rows // 2
    flip = (2 * col >= n_col).astype(jnp.int32)

    def mirrored(index, count):
        return flip * index + (1 - flip) * (count - 1 - index)

    def piece_of(slot, i, first=0, count=rows):
        lanes = pl.ds(pl.multiple_of(mirrored(i, chunks) * chunk, LANES), chunk)
        return image.at[pl.ds(slot * rows + first, count), lanes]

    image_copies = {}

    def send_image(name, src_slot, dst_slot, i, target, first=0, count=rows):
        image_copies[name, i] = remote(
            piece_of(src_slot, i, first, count),
            piece_of(dst_slot, i, first, count),
            image_send.at[name, i],
            image_recv.at[name, i],
            (target, col),
        )
        image_copies[name, i].start()

    def send_own(i):
        send_image(2, 0, 2, i, peer(1, 0))
        send_image(4, 0, 4, i, peer(2, 0))
        send_image(1, 0, 1, i, peer(0, 1))

    def pass_direct(i):
        image_copies[2, i].wait_recv()
        send_image(6, 2, 6, i, peer(2, 0), 0, half)
        send_image(3, 2, 3, i, peer(0, 1))
        image_copies[4, i].wait_recv()
        send_image(8, 4, 6, i, peer(1, 0), half, half)
        send_image(5, 4, 5, i, peer(0, 1))

    def pass_corner(i):
        image_copies[6, i].wait_recv()
        image_copies[8, i].wait_recv()
        send_image(7, 6, 7, i, peer(0, 1))

    for i in range(chunks - 1):
        send_own(i)

    def cross_text_piece(q, start, stop):
        return dot_nn(cross[q].T, embed[:, pl.ds(start, stop - start)])

    def store_cross(base, value):
        cross_text[:, pl.ds(base, LANES)] = value.astype(jnp.bfloat16)

    by_tile(cross_text_piece, bounds, store_cross)

    pass_direct(0)
    send_own(chunks - 1)
    pass_corner(0)
    for i in range(1, chunks):
        pass_direct(i)
    for i in range(1, chunks - 1):
        pass_corner(i)
    back_copy.start()

    main = head_cols // LANES * LANES
    tail = head_cols - main
    groups = head_rows // tail_rows

    def lanes_of(block):
        first = block * head_cols // LANES * LANES
        offset = block * head_cols - first
        part = total[:, pl.ds(pl.multiple_of(first, LANES), window)]
        return pltpu.roll(part, (window - offset) % window, 1)

    def packed(block):
        part = lanes_of(block)
        parts = [part[:, base : base + LANES] for base in range(0, main, LANES)]
        if tail:
            last = part[:, main : main + LANES]
            lane = lax.broadcasted_iota(jnp.int32, last.shape, 1)
            last = jnp.where(lane < tail, last, 0.0)
            joined = last[:tail_rows]
            for j in range(1, groups):
                here = last[j * tail_rows : (j + 1) * tail_rows]
                joined = joined + pltpu.roll(here, j * tail, 1)
            parts.append(joined)
        return parts

    def out_copy(block):
        return remote(
            sent.at[block],
            landed.at[col],
            out_send.at[block],
            out_recv.at[col],
            (row, block),
        )

    def in_copy(block):
        return remote(
            sent.at[block],
            landed.at[block],
            out_send.at[block],
            out_recv.at[block],
            (row, block),
        )

    for copy in pool_copies:
        copy.wait_recv()
    done = 0
    for i in range(chunks):
        if i == chunks - 1:
            pass_corner(i)
        image_copies[1, i].wait_recv()
        for slot in (3, 5, 7):
            image_copies[slot, i].wait_recv()
        lanes = pl.ds(pl.multiple_of(mirrored(i, chunks) * chunk, LANES), chunk)
        total[:, lanes] = dot_nn(pooled_cols[...], image[:, lanes])
        while done < n_col and ready[done] <= (i + 1) * chunk:
            block = mirrored(done, n_col)

            @pl.when(block != col)
            def _():
                at = 0
                for part in packed(block):
                    count = part.shape[0]
                    sent[block, pl.ds(at, count), :] = part.astype(jnp.bfloat16)
                    at += count
                out_copy(block).start()

            done += 1

    back_copy.wait_recv()
    text_grad_ref[...] = text_grad_ref[...] + text_back[...].astype(jnp.float32)

    results = packed(col)
    for d in range(n_col - 1, 0, -1):
        block = (col + d) % n_col
        in_copy(block).wait_recv()
        at = 0
        for n, part in enumerate(results):
            count = part.shape[0]
            got = landed[block, pl.ds(at, count), :]
            results[n] = part + got.astype(jnp.float32)
            at += count
    for n in range(main // LANES):
        head_grad_ref[:, pl.ds(n * LANES, LANES)] = results[n]
    if tail:
        for j in range(groups):
            here = results[-1]
            if j > 0:
                here = pltpu.roll(here, LANES - j * tail, 1)
            head_grad_ref[pl.ds(j * tail_rows, tail_rows), pl.ds(main, tail)] = here[:, :tail]

    behind_copy.wait_send()
    back_copy.wait_send()
    for copy in pool_copies:
        copy.wait_send()
    for name in sorted(image_copies):
        image_copies[name].wait_send()
    for d in range(1, n_col):
        in_copy((col + d) % n_col).wait_send()


def deliver(text_grad, head_grad):
    parts = 4
    step = text_grad.shape[0] // parts

    def move(text_from, head_from, text_to, head_to, text_held, head_held, sems, head_sems):
        def rows_of(ref, n):
            return ref.at[pl.ds(n * step, step), :]

        loads = [
            pltpu.make_async_copy(rows_of(text_from, n), rows_of(text_held, n), sems.at[0, n])
            for n in range(parts)
        ]
        head_load = pltpu.make_async_copy(head_from, head_held, head_sems.at[0])
        for load in loads:
            load.start()
        head_load.start()
        stores = []
        for n in range(parts):
            loads[n].wait()
            stores.append(
                pltpu.make_async_copy(rows_of(text_held, n), rows_of(text_to, n), sems.at[1, n])
            )
            stores[n].start()
        head_load.wait()
        head_store = pltpu.make_async_copy(head_held, head_to, head_sems.at[1])
        head_store.start()
        for store in stores:
            store.wait()
        head_store.wait()

    anywhere = pl.BlockSpec(memory_space=pl.ANY)
    return pl.pallas_call(
        move,
        out_shape=(
            jax.ShapeDtypeStruct(text_grad.shape, text_grad.dtype),
            jax.ShapeDtypeStruct(head_grad.shape, head_grad.dtype),
        ),
        in_specs=[anywhere, anywhere],
        out_specs=(anywhere, anywhere),
        scratch_shapes=[
            pltpu.VMEM(text_grad.shape, text_grad.dtype),
            pltpu.VMEM(head_grad.shape, head_grad.dtype),
            pltpu.SemaphoreType.DMA((2, parts)),
            pltpu.SemaphoreType.DMA((2,)),
        ],
    )(text_grad, head_grad)


def plan_of(width, n_row, n_col):
    head_rows, head_cols = width // n_row, width // n_col
    chunks = next((n for n in (3, 2, 1) if width % (n * LANES) == 0), None)
    spans = [aligned(c * head_cols, (c + 1) * head_cols) for c in range(n_col)]
    window = max(stop - start for start, stop in spans)
    starts = [start for start, _ in spans]
    if chunks is None or any(start + window > width for start in starts):
        return None
    ready = [
        max(starts[c] + window, width - starts[n_col - 1 - c]) for c in range(n_col)
    ]
    tail = head_cols % LANES
    fitting = [
        n
        for n in range(1, LANES // tail + 1 if tail else 2)
        if head_rows % (16 * n) == 0
    ]
    if not fitting or head_cols < LANES:
        return None
    return chunks, ready, window, head_rows // max(fitting)


def fused_body(n_row, n_col, pooled, text_embed, head_weight, logit_scale, logit_bias, partner):
    rows, width = pooled.shape
    factor = 1.0 / math.sqrt(rows * n_row * n_col)
    chunks, ready, window, tail_rows = plan_of(width, n_row, n_col)
    head_cols = width // n_col
    packed_rows = head_cols // LANES * (width // n_row)
    packed_rows += tail_rows if head_cols % LANES else 0
    bounds = [0, width // 8, width // 4, width // 2, width]
    spans = [aligned(bounds[q], bounds[q + 1]) for q in range(4)]
    masked_width = sum(stop - start for start, stop in spans)
    head_rows, head_cols = width // n_row, width // n_col
    vmem = pl.BlockSpec(memory_space=pltpu.VMEM)
    smem = pl.BlockSpec(memory_space=pltpu.SMEM)
    dma = pltpu.SemaphoreType.DMA
    return pl.pallas_call(
        functools.partial(
            kernel, n_row, n_col, factor, chunks, ready, window, tail_rows
        ),
        out_shape=(
            jax.ShapeDtypeStruct((rows, width), jnp.float32),
            jax.ShapeDtypeStruct((head_rows, head_cols), jnp.float32),
        ),
        in_specs=[vmem, vmem, pl.BlockSpec(memory_space=pl.ANY), smem, smem, vmem],
        out_specs=(vmem, vmem),
        scratch_shapes=[
            pltpu.VMEM(head_weight.shape, jnp.bfloat16),
            dma,
            pltpu.VMEM((rows, width), jnp.float32),
            pltpu.VMEM((rows, width), jnp.bfloat16),
            pltpu.VMEM((rows, width), jnp.bfloat16),
            pltpu.VMEM((rows, width), jnp.bfloat16),
            pltpu.VMEM((width, rows), jnp.bfloat16),
            pltpu.VMEM((head_rows, n_row * rows), jnp.bfloat16),
            pltpu.VMEM((rows, width), jnp.bfloat16),
            pltpu.VMEM((rows, masked_width), jnp.bfloat16),
            pltpu.VMEM((n_row * rows, width), jnp.bfloat16),
            pltpu.VMEM((head_rows, width), jnp.float32),
            pltpu.VMEM((n_col, packed_rows, LANES), jnp.bfloat16),
            pltpu.VMEM((n_col, packed_rows, LANES), jnp.bfloat16),
            dma((2,)),
            dma((2,)),
            dma((n_row,)),
            dma((n_row,)),
            dma((n_row + 1, chunks)),
            dma((n_row + 1, chunks)),
            dma((n_col,)),
            dma((n_col,)),
        ],
        compiler_params=pltpu.CompilerParams(collective_id=0, has_side_effects=True),
    )(pooled, text_embed, head_weight, logit_scale, logit_bias, partner)


def per_device(n_row, n_col):
    def run(pooled, text_embed, head_weight, logit_scale, logit_bias, partner):
        rows, width = pooled.shape
        fused = (
            n_row == 2**3
            and n_col > 1
            and rows == LANES
            and width % LANES == 0
            and width % (16 * n_row) == 0
            and width % n_col == 0
            and plan_of(width, n_row, n_col) is not None
        )
        args = (pooled, text_embed, head_weight, logit_scale, logit_bias, partner)
        return deliver(*fused_body(n_row, n_col, *args)) if fused else body(*args)

    return run


def solution(mesh):
    in_specs = (
        P(("row", "col"), None),
        P(("row", "col"), None),
        P(),
        P(),
        P(),
        P(("row", "col"), None),
    )
    out_specs = (P(("row", "col"), None), P("row", "col"))
    run = per_device(mesh.shape["row"], mesh.shape["col"])
    return jax.shard_map(run, mesh=mesh, in_specs=in_specs, out_specs=out_specs, check_vma=False)
```

profile of v0, /device:TPU:0, one launch (start us, length us, event | category | flops | bytes accessed | tf_op | source)
XLA Modules:
  0.0 36.4 jit_solution(14998771768816839862)
XLA Ops:
  0.6 33.8 %shard_map.77 = (f32[128,1152]{1,0:T(8,128)}, f32[144,288]{1,0:T(8,128)}) custom-call(bf16[128,1152]{1,0:T(8,128)(2,1)} %pooled_ref.1, bf16[128,1152]{1,0:T(8,128)(2,1)} %text_ref.1, bf16[1152,1152]{1,0:T(8,128)(2,1)} %weight_hbm.1, f32[4]{0:T(128)} %scale_ref.1, f32[4]{0:T(128)} %bias_ref.1, s32[1,128]{1,0:T(1,128)} %partner_ref.1), custom_call_target="tpu_custom_call" | custom-call | tf_op jit(solution)/shard_map/pallas_call | solution.py:593
  34.4 2.0 %shard_map.78 = (f32[128,1152]{1,0:T(8,128)}, f32[144,288]{1,0:T(8,128)}) custom-call(f32[128,1152]{1,0:T(8,128)} %get-tuple-element.4.text_from, f32[144,288]{1,0:T(8,128)} %get-tuple-element.5.head_from), custom_call_target="tpu_custom_call" | custom-call | tf_op jit(solution)/shard_map/pallas_call | solution.py:540
where the time goes:
time: 36.6 us; the launch traced here: 36.4 us
  Pallas kernels  35.8 us (98%)
  between operations  0.64 us (2%)
    pallas_call x1, Pallas kernels, fused_body(): pl.pallas_call(functools.partial(kernel, n_row, n_col, factor, chunks, re...  33.8 us
    pallas_call x1, Pallas kernels, deliver(): pl.pallas_call(move, out_shape=(jax.ShapeDtypeStruct(text_grad.shape, tex...  2 us

commit v1 on v0

--- a/solution.py
+++ b/solution.py
@@ -159,16 +159,21 @@
     ready,
     window,
     tail_rows,
+    pooled_hbm,
+    text_hbm,
+    weight_hbm,
+    scale_hbm,
+    bias_hbm,
+    partner_hbm,
+    text_grad_ref,
+    head_grad_ref,
     pooled_ref,
     text_ref,
-    weight_hbm,
+    weight_ref,
     scale_ref,
     bias_ref,
     partner_ref,
-    text_grad_ref,
-    head_grad_ref,
-    weight_ref,
-    weight_sem,
+    load_sem,
     image_own,
     cross_text,
     text_back,
@@ -190,7 +195,7 @@
     out_send,
     out_recv,
 ):
-    rows, width = pooled_ref.shape
+    rows, width = pooled_hbm.shape
     chips = n_row // 2
     head_rows = width // n_row
     head_cols = width // n_col
@@ -207,9 +212,6 @@
         there = chip + (k % 2) * (1 - 2 * side) + (k // 2) * (2 - 4 * level)
         return there * 2 + (core if e == 0 else 1 - core)
 
-    weight_copy = pltpu.make_async_copy(weight_hbm, weight_ref, weight_sem)
-    weight_copy.start()
-
     barrier = pltpu.get_barrier_semaphore()
     for d in range(1, n_row):
         pl.semaphore_signal(
@@ -219,6 +221,22 @@
         pl.semaphore_signal(
             barrier, inc=1, device_id=(row, (col + d) % n_col), device_id_type=MESH
         )
+
+    loads = [
+        pltpu.make_async_copy(src, dst, load_sem.at[n])
+        for n, (src, dst) in enumerate(
+            (
+                (pooled_hbm, pooled_ref),
+                (weight_hbm, weight_ref),
+                (text_hbm, text_ref),
+                (scale_hbm, scale_ref),
+                (bias_hbm, bias_ref),
+                (partner_hbm, partner_ref),
+            )
+        )
+    ]
+    for load in loads:
+        load.start()
 
     def remote(src, dst, send, recv, device):
         return pltpu.make_async_remote_copy(
@@ -231,7 +249,7 @@
         )
 
     behind_copy = remote(
-        text_ref, text_behind, near_send.at[0], near_recv.at[0], ((row + 1) % n_row, col)
+        text_hbm, text_behind, near_send.at[0], near_recv.at[0], ((row + 1) % n_row, col)
     )
     back_copy = remote(
         cross_text,
@@ -242,6 +260,7 @@
     )
     pl.semaphore_wait(barrier, n_row + n_col - 2)
     behind_copy.start()
+    loads[0].wait()
 
     for tile in range(width // LANES):
         lanes = pl.ds(tile * LANES, LANES)
@@ -299,8 +318,10 @@
 
     for copy in pool_copies:
         copy.start()
-    weight_copy.wait()
+    loads[1].wait()
     fill_embed(pooled_ref)
+    for load in loads[2:]:
+        load.wait()
     text_id = lax.broadcasted_iota(jnp.int32, (rows, rows), 0)
     positive = (text_id == partner_ref[...]).astype(jnp.float32).T
     own = weights_of(
@@ -507,35 +528,17 @@
 
 
 def deliver(text_grad, head_grad):
-    parts = 4
-    step = text_grad.shape[0] // parts
-
-    def move(text_from, head_from, text_to, head_to, text_held, head_held, sems, head_sems):
-        def rows_of(ref, n):
-            return ref.at[pl.ds(n * step, step), :]
-
-        loads = [
-            pltpu.make_async_copy(rows_of(text_from, n), rows_of(text_held, n), sems.at[0, n])
-            for n in range(parts)
+    def move(text_from, head_from, text_to, head_to, sems):
+        copies = [
+            pltpu.make_async_copy(text_from, text_to, sems.at[0]),
+            pltpu.make_async_copy(head_from, head_to, sems.at[1]),
         ]
-        head_load = pltpu.make_async_copy(head_from, head_held, head_sems.at[0])
-        for load in loads:
-            load.start()
-        head_load.start()
-        stores = []
-        for n in range(parts):
-            loads[n].wait()
-            stores.append(
-                pltpu.make_async_copy(rows_of(text_held, n), rows_of(text_to, n), sems.at[1, n])
-            )
-            stores[n].start()
-        head_load.wait()
-        head_store = pltpu.make_async_copy(head_held, head_to, head_sems.at[1])
-        head_store.start()
-        for store in stores:
-            store.wait()
-        head_store.wait()
-
+        for copy in copies:
+            copy.start()
+        for copy in copies:
+            copy.wait()
+
+    vmem = pl.BlockSpec(memory_space=pltpu.VMEM)
     anywhere = pl.BlockSpec(memory_space=pl.ANY)
     return pl.pallas_call(
         move,
@@ -543,15 +546,13 @@
             jax.ShapeDtypeStruct(text_grad.shape, text_grad.dtype),
             jax.ShapeDtypeStruct(head_grad.shape, head_grad.dtype),
         ),
-        in_specs=[anywhere, anywhere],
+        in_specs=[vmem, vmem],
         out_specs=(anywhere, anywhere),
-        scratch_shapes=[
-            pltpu.VMEM(text_grad.shape, text_grad.dtype),
-            pltpu.VMEM(head_grad.shape, head_grad.dtype),
-            pltpu.SemaphoreType.DMA((2, parts)),
-            pltpu.SemaphoreType.DMA((2,)),
-        ],
-    )(text_grad, head_grad)
+        scratch_shapes=[pltpu.SemaphoreType.DMA((2,))],
+    )(
+        pltpu.with_memory_space_constraint(text_grad, pltpu.VMEM),
+        pltpu.with_memory_space_constraint(head_grad, pltpu.VMEM),
+    )
 
 
 def plan_of(width, n_row, n_col):
@@ -588,21 +589,25 @@
     masked_width = sum(stop - start for start, stop in spans)
     head_rows, head_cols = width // n_row, width // n_col
     vmem = pl.BlockSpec(memory_space=pltpu.VMEM)
-    smem = pl.BlockSpec(memory_space=pltpu.SMEM)
     dma = pltpu.SemaphoreType.DMA
     return pl.pallas_call(
         functools.partial(
             kernel, n_row, n_col, factor, chunks, ready, window, tail_rows
         ),
         out_shape=(
-            jax.ShapeDtypeStruct((rows, width), jnp.float32),
-            jax.ShapeDtypeStruct((head_rows, head_cols), jnp.float32),
+            pltpu.VMEM((rows, width), jnp.float32),
+            pltpu.VMEM((head_rows, head_cols), jnp.float32),
         ),
-        in_specs=[vmem, vmem, pl.BlockSpec(memory_space=pl.ANY), smem, smem, vmem],
+        in_specs=[pl.BlockSpec(memory_space=pl.ANY)] * 6,
         out_specs=(vmem, vmem),
         scratch_shapes=[
+            pltpu.VMEM(pooled.shape, jnp.bfloat16),
+            pltpu.VMEM(text_embed.shape, jnp.bfloat16),
             pltpu.VMEM(head_weight.shape, jnp.bfloat16),
-            dma,
+            pltpu.SMEM(logit_scale.shape, jnp.float32),
+            pltpu.SMEM(logit_bias.shape, jnp.float32),
+            pltpu.VMEM(partner.shape, jnp.int32),
+            dma((6,)),
             pltpu.VMEM((rows, width), jnp.float32),
             pltpu.VMEM((rows, width), jnp.bfloat16),
             pltpu.VMEM((rows, width), jnp.bfloat16),

time: 36.6 us -> 33.6 us (0.918)
  Pallas kernels: 35.8 us -> 32.8 us
    pallas_call x1, Pallas kernels: 33.8 us -> 31.9 us  [fused_body(): pl.pallas_call(functools.partial(kernel, n_row, n_col, factor, chunks, re...]
    pallas_call x1, Pallas kernels: 2 us -> 0.9 us  [deliver(): pl.pallas_call(move, out_shape=(jax.ShapeDtypeStruct(text_grad.shape, tex...]
where the time goes in v1:
time: 33.6 us; the launch traced here: 33.5 us
  Pallas kernels  32.8 us (98%)
  between operations  0.64 us (2%)
    pallas_call x1, Pallas kernels, fused_body(): pl.pallas_call(functools.partial(kernel, n_row, n_col, factor, chunks, re...  31.9 us
    pallas_call x1, Pallas kernels, deliver(): pl.pallas_call(move, out_shape=(jax.ShapeDtypeStruct(text_grad.shape, tex...  0.9 us

profile of v1, /device:TPU:0, one launch (start us, length us, event | category | flops | bytes accessed | tf_op | source)
XLA Modules:
  0.0 33.5 jit_solution(7785776340733340528)
XLA Ops:
  0.6 31.9 %shard_map.77 = (f32[128,1152]{1,0:T(8,128)S(1)}, f32[144,288]{1,0:T(8,128)S(1)}) custom-call(bf16[128,1152]{1,0:T(8,128)(2,1)} %pooled_hbm.1, bf16[128,1152]{1,0:T(8,128)(2,1)} %text_hbm.1, bf16[1152,1152]{1,0:T(8,128)(2,1)} %weight_hbm.1, f32[4]{0:T(128)} %scale_hbm.1, f32[4]{0:T(128)} %bias_hbm.1, s32[1,128]{1,0:T(1,128)} %partner_hbm.1), custom_call_target="tpu_custom_call" | custom-call | tf_op jit(solution)/shard_map/pallas_call | solution.py:593
  32.6 0.9 %shard_map.78 = (f32[128,1152]{1,0:T(8,128)}, f32[144,288]{1,0:T(8,128)}) custom-call(f32[128,1152]{1,0:T(8,128)S(1)} %get-tuple-element.4.text_from, f32[144,288]{1,0:T(8,128)S(1)} %get-tuple-element.5.head_from), custom_call_target="tpu_custom_call" | custom-call | tf_op jit(solution)/shard_map/pallas_call | solution.py:543

commit v2 on v1

v2 whole, which is shorter than its diff:
```python
import functools
import math

import jax
import jax.numpy as jnp
from jax import lax
from jax.experimental import pallas as pl
from jax.experimental.pallas import tpu as pltpu
from jax.sharding import PartitionSpec as P

LANES = 128
MESH = pl.DeviceIdType.MESH


def shifted(value, axis, by):
    count = lax.axis_size(axis)
    return lax.ppermute(value, axis, [(i, (i + by) % count) for i in range(count)])


def segment_weights(image_part, text_part, positive, logit_scale, logit_bias, factor):
    model_width = image_part.shape[1]
    bounds = [0, model_width // 8, model_width // 4, model_width // 2, model_width]
    running = jnp.zeros((image_part.shape[0], text_part.shape[0]), jnp.float32)
    level_grads = []
    for prefix in range(4):
        low_end = bounds[prefix]
        high_end = bounds[prefix + 1]
        running = running + jnp.dot(
            image_part[:, low_end:high_end],
            text_part[:, low_end:high_end].T,
            preferred_element_type=jnp.float32,
        )
        logits = logit_scale[prefix] * running + logit_bias[prefix]
        level_grads.append((jax.nn.sigmoid(logits) - positive) * factor)
    weights = []
    carried = jnp.zeros_like(running)
    for prefix in range(3, -1, -1):
        carried = carried + logit_scale[prefix] * level_grads[prefix]
        weights.insert(0, carried.astype(jnp.bfloat16))
    return (weights, bounds)


def image_side(weights, bounds, text_part):
    pieces = []
    for prefix in range(4):
        pieces.append(
            jnp.dot(
                weights[prefix],
                text_part[:, bounds[prefix] : bounds[prefix + 1]],
                preferred_element_type=jnp.float32,
            )
        )
    return jnp.concatenate(pieces, 1)


def text_side(weights, bounds, image_part):
    pieces = []
    for prefix in range(4):
        pieces.append(
            jnp.dot(
                weights[prefix].T,
                image_part[:, bounds[prefix] : bounds[prefix + 1]],
                preferred_element_type=jnp.float32,
            )
        )
    return jnp.concatenate(pieces, 1)


def body(pooled, text_embed, head_weight, logit_scale, logit_bias, partner):
    block_rows = pooled.shape[0]
    factor = 1.0 / math.sqrt(block_rows * lax.axis_size("row") * lax.axis_size("col"))
    embedding = jnp.dot(pooled, head_weight, preferred_element_type=jnp.float32).astype(
        jnp.bfloat16
    )
    local_ids = jnp.arange(block_rows, dtype=jnp.int32)
    positive = (partner[0][:, None] == local_ids[None, :]).astype(jnp.float32)
    empty = jnp.zeros((block_rows, block_rows), jnp.float32)
    weights, bounds = segment_weights(
        embedding, text_embed, positive, logit_scale, logit_bias, factor
    )
    own_image = image_side(weights, bounds, text_embed)
    own_text = text_side(weights, bounds, embedding)
    behind = shifted(text_embed, "row", 1)
    weights, bounds = segment_weights(embedding, behind, empty, logit_scale, logit_bias, factor)
    cross_image = image_side(weights, bounds, behind)
    cross_text = text_side(weights, bounds, embedding)
    returned = shifted(cross_text.astype(jnp.bfloat16), "row", -1).astype(cross_text.dtype)
    text_grad = own_text + returned
    image_grad = own_image + cross_image
    column_block = lax.all_to_all(
        image_grad.astype(jnp.bfloat16), "col", split_axis=1, concat_axis=0, tiled=True
    ).astype(image_grad.dtype)
    group_rows = lax.all_gather(pooled, "col", axis=0, tiled=True)
    block_term = jnp.dot(
        group_rows.astype(jnp.float32).T, column_block, precision=lax.Precision.HIGHEST
    )
    head_grad = lax.psum_scatter(block_term, "row", scatter_dimension=0, tiled=True)
    return (text_grad, head_grad)


def dot_nt(left, right):
    return lax.dot_general(
        left, right, (((1,), (1,)), ((), ())), preferred_element_type=jnp.float32
    )


def dot_nn(left, right):
    return jnp.dot(left, right, preferred_element_type=jnp.float32)


def aligned(low_end, high_end):
    return low_end // LANES * LANES, -(-high_end // LANES) * LANES


def weights_of(score_of, positive, scale_ref, bias_ref, factor):
    running = None
    level_grads = []
    for prefix in range(4):
        part = score_of(prefix)
        running = part if running is None else running + part
        gate = jax.nn.sigmoid(scale_ref[prefix] * running + bias_ref[prefix])
        if positive is not None:
            gate = gate - positive
        level_grads.append(gate * factor)
    weights = [None] * 4
    carried = None
    for prefix in range(3, -1, -1):
        term = scale_ref[prefix] * level_grads[prefix]
        carried = term if carried is None else carried + term
        weights[prefix] = carried.astype(jnp.bfloat16)
    return weights


def by_tile(piece_of, bounds, store):
    pieces = []
    for q in range(4):
        start, stop = aligned(bounds[q], bounds[q + 1])
        pieces.append((start, stop, piece_of(q, start, stop)))
    for tile in range(bounds[4] // LANES):
        base = tile * LANES
        value = None
        for q in range(4):
            start, stop, piece = pieces[q]
            if start <= base < stop:
                here = piece[:, base - start : base - start + LANES]
                if value is None:
                    value = here
                else:
                    lane = lax.broadcasted_iota(jnp.int32, here.shape, 1)
                    value = jnp.where(lane < bounds[q] - base, value, here)
        store(base, value)


def kernel(
    n_row,
    n_col,
    factor,
    plan,
    pooled_hbm,
    text_hbm,
    weight_hbm,
    scale_hbm,
    bias_hbm,
    partner_hbm,
    text_grad_ref,
    head_grad_ref,
    pooled_ref,
    text_ref,
    weight_ref,
    scale_ref,
    bias_ref,
    partner_ref,
    load_sem,
    image_sum,
    cross_text,
    text_back,
    text_behind,
    pooled_t,
    pooled_in,
    embed,
    masked,
    image_out,
    image_in,
    total,
    x_out,
    x_in,
    z_out,
    z_in,
    near_send,
    near_recv,
    pool_send,
    pool_recv,
    image_send,
    image_recv,
    x_send,
    x_recv,
    z_send,
    z_recv,
):
    window, image_tail, out_tail = plan
    rows, width = pooled_hbm.shape
    head_rows = width // n_row
    head_cols = width // n_col
    tiles = head_cols // LANES
    tail = head_cols % LANES
    bounds = [0, width // 8, width // 4, width // 2, width]
    row = lax.axis_index("row")
    col = lax.axis_index("col")
    half = n_row // 2
    y = row // half
    x = row // 2 % 2
    core = row % 2
    pair = col % 2
    side = col // 2

    other_core = row + 1 - 2 * core
    over_y = (row + half) % n_row
    over_y_other = over_y + 1 - 2 * core
    over_x = row + 2 - 4 * x
    over_z = col + 1 - 2 * pair
    far_z = (col + 2) % n_col

    barrier = pltpu.get_barrier_semaphore()
    peers = (
        ((row + 1) % n_row, col),
        ((row + n_row - 1) % n_row, col),
        (over_x, col),
        (over_y, col),
        (over_y_other, col),
        (row, over_z),
        (other_core, over_z),
        (row, far_z),
    )
    for peer in peers:
        pl.semaphore_signal(barrier, inc=1, device_id=peer, device_id_type=MESH)

    loads = [
        pltpu.make_async_copy(src, dst, load_sem.at[n])
        for n, (src, dst) in enumerate(
            (
                (pooled_hbm, pooled_ref),
                (weight_hbm, weight_ref),
                (text_hbm, text_ref),
                (scale_hbm, scale_ref),
                (bias_hbm, bias_ref),
                (partner_hbm, partner_ref),
            )
        )
    ]
    for load in loads:
        load.start()

    def remote(src, dst, send, recv, device):
        return pltpu.make_async_remote_copy(
            src_ref=src,
            dst_ref=dst,
            send_sem=send,
            recv_sem=recv,
            device_id=device,
            device_id_type=MESH,
        )

    behind_copy = remote(
        text_hbm, text_behind, near_send.at[0], near_recv.at[0], ((row + 1) % n_row, col)
    )
    back_copy = remote(
        cross_text,
        text_back,
        near_send.at[1],
        near_recv.at[1],
        ((row + n_row - 1) % n_row, col),
    )
    pl.semaphore_wait(barrier, len(peers))
    behind_copy.start()
    loads[0].wait()

    for tile in range(width // LANES):
        part = pooled_ref[:, pl.ds(tile * LANES, LANES)].T
        at = tile * LANES
        while at < (tile + 1) * LANES:
            block = at // head_rows
            stop = min((block + 1) * head_rows, (tile + 1) * LANES)
            pooled_t[block // 2, block % 2, pl.ds(at - block * head_rows, stop - at), :] = part[
                at - tile * LANES : stop - tile * LANES
            ]
            at = stop

    def pool_copy(src, slot, device):
        return remote(src, pooled_in.at[slot], pool_send.at[slot], pool_recv.at[slot], device)

    def pooled_for(half_y, half_core):
        return pooled_t.at[pl.ds(2 * half_y, 2), half_core]

    pool_copies = {
        4: pool_copy(pooled_for(y, core), 4, (row, over_z)),
        5: pool_copy(pooled_for(y, 1 - core), 5, (other_core, over_z)),
        2: pool_copy(pooled_for(1 - y, core), 2, (over_y, col)),
        3: pool_copy(pooled_for(1 - y, 1 - core), 3, (over_y_other, col)),
        1: pool_copy(pooled_for(y, 1 - core), 1, (other_core, col)),
    }
    for copy in pool_copies.values():
        copy.start()
    for slot in (6, 7):
        pool_copies[slot] = pool_copy(pooled_in.at[slot - 4], slot, (row, over_z))
    pooled_in[0] = pooled_t[pl.ds(2 * y, 2), core]

    def fill_embed(source):
        at = 0
        for q in range(4):
            start, stop = aligned(bounds[q], bounds[q + 1])
            at += stop - start
        step = 3 * LANES if width % (3 * LANES) == 0 else LANES
        for base in range(0, width, step):
            part = dot_nn(source[...], weight_ref[:, pl.ds(base, step)])
            embed[:, pl.ds(base, step)] = part.astype(jnp.bfloat16)
        at = 0
        for q in range(4):
            start, stop = aligned(bounds[q], bounds[q + 1])
            part = embed[:, pl.ds(start, stop - start)].astype(jnp.float32)
            lane = lax.broadcasted_iota(jnp.int32, part.shape, 1) + start
            keep = (lane >= bounds[q]) & (lane < bounds[q + 1])
            masked[:, pl.ds(at, stop - start)] = jnp.where(keep, part, 0.0).astype(
                jnp.bfloat16
            )
            at += stop - start

    def masked_part(q):
        at = 0
        for before in range(q):
            start, stop = aligned(bounds[before], bounds[before + 1])
            at += stop - start
        start, stop = aligned(bounds[q], bounds[q + 1])
        return masked[:, pl.ds(at, stop - start)]

    def text_part(ref, q):
        start, stop = aligned(bounds[q], bounds[q + 1])
        return ref[:, pl.ds(start, stop - start)]

    loads[1].wait()
    fill_embed(pooled_ref)
    for load in loads[2:]:
        load.wait()
    text_id = lax.broadcasted_iota(jnp.int32, (rows, rows), 0)
    positive = (text_id == partner_ref[...]).astype(jnp.float32).T
    own = weights_of(
        lambda q: dot_nt(masked_part(q), text_part(text_ref, q)),
        positive,
        scale_ref,
        bias_ref,
        factor,
    )

    def own_image_piece(q, start, stop):
        return dot_nn(own[q], text_ref[:, pl.ds(start, stop - start)])

    def keep_image(base, value):
        image_sum[:, pl.ds(base, LANES)] = value

    by_tile(own_image_piece, bounds, keep_image)

    def folded(value, kept):
        lane = lax.broadcasted_iota(jnp.int32, value.shape, 1)
        value = jnp.where(lane < tail, value, 0.0)
        joined = value[:kept]
        for n in range(1, value.shape[0] // kept):
            joined = joined + pltpu.roll(value[n * kept : (n + 1) * kept], n * tail, 1)
        return joined

    def block_of(turn, parity):
        return parity + 2 * (side if turn == 1 else 1 - side)

    def image_copy(src, slot, turn, device):
        return remote(
            src,
            image_in.at[turn, slot],
            image_send.at[slot, turn],
            image_recv.at[slot, turn],
            device,
        )

    image_copies = {}
    for turn in range(2):
        mine = image_out.at[block_of(turn, pair)]
        theirs = image_out.at[block_of(turn, 1 - pair)]
        held = [image_in.at[turn, slot] for slot in range(8)]
        image_copies[4, turn] = image_copy(theirs, 4, turn, (row, over_z))
        image_copies[2, turn] = image_copy(mine, 2, turn, (over_y, col))
        image_copies[1, turn] = image_copy(mine, 1, turn, (other_core, col))
        image_copies[6, turn] = image_copy(held[4], 6, turn, (over_y, col))
        for slot in (3, 5, 7):
            image_copies[slot, turn] = image_copy(held[slot - 1], slot, turn, (other_core, col))

    def cross_phase():
        behind_copy.wait_recv()
        cross = weights_of(
            lambda q: dot_nt(masked_part(q), text_part(text_behind, q)),
            None,
            scale_ref,
            bias_ref,
            factor,
        )

        def image_piece(q, start, stop):
            return dot_nn(cross[q], text_behind[:, pl.ds(start, stop - start)])

        def add_image(base, value):
            lanes = pl.ds(base, LANES)
            image_sum[:, lanes] = image_sum[:, lanes] + value

        by_tile(image_piece, bounds, add_image)
        for block in range(n_col):
            first = block * head_cols // LANES * LANES
            offset = block * head_cols - first
            part = image_sum[:, pl.ds(first, window)]
            if offset:
                part = pltpu.roll(part, window - offset, 1)
            for n in range(tiles):
                image_out[block, pl.ds(n * rows, rows), :] = part[
                    :, n * LANES : (n + 1) * LANES
                ].astype(jnp.bfloat16)
            if tail:
                last = folded(part[:, tiles * LANES : (tiles + 1) * LANES], image_tail)
                image_out[block, pl.ds(tiles * rows, image_tail), :] = last.astype(jnp.bfloat16)
        for turn in range(2):
            for slot in (4, 2, 1):
                image_copies[slot, turn].start()

        def own_text_piece(q, start, stop):
            return dot_nn(own[q].T, embed[:, pl.ds(start, stop - start)])

        def store_text(base, value):
            text_grad_ref[:, pl.ds(base, LANES)] = value

        def cross_text_piece(q, start, stop):
            return dot_nn(cross[q].T, embed[:, pl.ds(start, stop - start)])

        def store_cross(base, value):
            cross_text[:, pl.ds(base, LANES)] = value.astype(jnp.bfloat16)

        by_tile(cross_text_piece, bounds, store_cross)
        back_copy.start()
        by_tile(own_text_piece, bounds, store_text)

    pl.when(core == 1)(cross_phase)
    for slot in (6, 7):
        pool_copies[slot - 4].wait_recv()
        pool_copies[slot].start()
    pl.when(core == 0)(cross_phase)

    for turn in range(2):
        image_in[turn, 0] = image_out[block_of(turn, pair)]

    def forward(slot, turn):
        image_copies[slot, turn].wait_recv()
        if slot == 4:
            image_copies[6, turn].start()
        image_copies[slot + 1, turn].start()

    for turn in range(2):
        forward(4, turn)
        forward(2, turn)
    forward(6, 0)
    for slot in (1, 4, 5, 6, 7):
        pool_copies[slot].wait_recv()

    parts = [(n * head_rows, head_rows) for n in range(tiles)]
    if tail:
        parts.append((tiles * head_rows, out_tail))

    def part_of(ref, n):
        return ref.at[pl.ds(parts[n][0], parts[n][1]), :]

    x_copies = {
        (turn, n): remote(
            part_of(x_out.at[turn], n),
            part_of(x_in.at[turn], n),
            x_send.at[turn, n],
            x_recv.at[turn, n],
            (over_x, col),
        )
        for turn in range(2)
        for n in range(len(parts))
    }
    z_copies = [
        remote(part_of(z_out, n), part_of(z_in, n), z_send.at[n], z_recv.at[n], (row, far_z))
        for n in range(len(parts))
    ]

    def keep_part(turn, n, value):
        first, count = parts[n]
        for there in range(2):
            piece = value[there * head_rows : (there + 1) * head_rows]
            if n == tiles:
                piece = folded(piece, count)
            total[turn, there, pl.ds(first, count), :] = piece
        x_out[turn, pl.ds(first, count), :] = total[
            turn, 1 - x, pl.ds(first, count), :
        ].astype(jnp.bfloat16)
        x_copies[turn, n].start()

    def multiply(turn):
        for slot in (1, 3, 5, 7):
            image_copies[slot, turn].wait_recv()
        left = jnp.concatenate(
            [pooled_in[slot].reshape(2 * head_rows, rows) for slot in range(8)], 1
        )
        sides = [
            image_in[turn, :, pl.ds(n * rows, rows), :].reshape(8 * rows, LANES)
            for n in range(tiles)
        ]
        main = dot_nn(left, jnp.concatenate(sides, 1))
        for n in range(tiles):
            keep_part(turn, n, main[:, n * LANES : (n + 1) * LANES])
        if tail:
            pieces = []
            for slot in range(8):
                held = image_in[turn, slot, pl.ds(tiles * rows, image_tail), :]
                held = held.astype(jnp.float32)
                for n in range(rows // image_tail):
                    moved = pltpu.roll(held, LANES - n * tail, 1) if n else held
                    pieces.append(moved.astype(jnp.bfloat16))
            keep_part(turn, tiles, dot_nn(left, jnp.concatenate(pieces, 0)))

    @pl.when(core == 1)
    def _():
        forward(6, 1)

    multiply(0)

    @pl.when(core == 0)
    def _():
        forward(6, 1)

    multiply(1)
    for n, (first, count) in enumerate(parts):
        at = pl.ds(first, count)
        x_copies[0, n].wait_recv()
        value = total[0, x, at, :] + x_in[0, at, :].astype(jnp.float32)
        z_out[at, :] = value.astype(jnp.bfloat16)
        z_copies[n].start()

    back_copy.wait_recv()
    text_grad_ref[...] = text_grad_ref[...] + text_back[...].astype(jnp.float32)

    for n, (first, count) in enumerate(parts):
        at = pl.ds(first, count)
        x_copies[1, n].wait_recv()
        value = total[1, x, at, :] + x_in[1, at, :].astype(jnp.float32)
        z_copies[n].wait_recv()
        value = value + z_in[at, :].astype(jnp.float32)
        if n < tiles:
            head_grad_ref[:, pl.ds(n * LANES, LANES)] = value
        else:
            for j in range(head_rows // count):
                here = pltpu.roll(value, LANES - j * tail, 1) if j else value
                head_grad_ref[pl.ds(j * count, count), pl.ds(tiles * LANES, tail)] = here[:, :tail]

    behind_copy.wait_send()
    back_copy.wait_send()
    for copies in (pool_copies, image_copies, x_copies):
        for name in sorted(copies):
            copies[name].wait_send()
    for copy in z_copies:
        copy.wait_send()


def deliver(text_grad, head_grad):
    def move(text_from, head_from, text_to, head_to, sems):
        copies = [
            pltpu.make_async_copy(text_from, text_to, sems.at[0]),
            pltpu.make_async_copy(head_from, head_to, sems.at[1]),
        ]
        for copy in copies:
            copy.start()
        for copy in copies:
            copy.wait()

    vmem = pl.BlockSpec(memory_space=pltpu.VMEM)
    anywhere = pl.BlockSpec(memory_space=pl.ANY)
    return pl.pallas_call(
        move,
        out_shape=(
            jax.ShapeDtypeStruct(text_grad.shape, text_grad.dtype),
            jax.ShapeDtypeStruct(head_grad.shape, head_grad.dtype),
        ),
        in_specs=[vmem, vmem],
        out_specs=(anywhere, anywhere),
        scratch_shapes=[pltpu.SemaphoreType.DMA((2,))],
    )(
        pltpu.with_memory_space_constraint(text_grad, pltpu.VMEM),
        pltpu.with_memory_space_constraint(head_grad, pltpu.VMEM),
    )


def fold_of(count, tail):
    fitting = [n for n in range(1, LANES // tail + 1 if tail else 2) if count % (16 * n) == 0]
    return count // max(fitting) if fitting else None


def plan_of(rows, width, n_row, n_col):
    head_rows, head_cols = width // n_row, width // n_col
    spans = [aligned(c * head_cols, (c + 1) * head_cols) for c in range(n_col)]
    window = max(stop - start for start, stop in spans)
    if head_cols < LANES or any(start + window > width for start, _ in spans):
        return None
    image_tail = fold_of(rows, head_cols % LANES)
    out_tail = fold_of(head_rows, head_cols % LANES)
    if image_tail is None or out_tail is None:
        return None
    return window, image_tail, out_tail


def fused_body(n_row, n_col, pooled, text_embed, head_weight, logit_scale, logit_bias, partner):
    rows, width = pooled.shape
    factor = 1.0 / math.sqrt(rows * n_row * n_col)
    plan = plan_of(rows, width, n_row, n_col)
    _, image_tail, out_tail = plan
    head_rows, head_cols = width // n_row, width // n_col
    tiles, ragged = head_cols // LANES, head_cols % LANES > 0
    image_rows = tiles * rows + ragged * image_tail
    out_rows = tiles * head_rows + ragged * out_tail
    parts = tiles + ragged
    bounds = [0, width // 8, width // 4, width // 2, width]
    spans = [aligned(bounds[q], bounds[q + 1]) for q in range(4)]
    masked_width = sum(stop - start for start, stop in spans)
    vmem = pl.BlockSpec(memory_space=pltpu.VMEM)
    dma = pltpu.SemaphoreType.DMA
    bf16, f32 = jnp.bfloat16, jnp.float32
    return pl.pallas_call(
        functools.partial(kernel, n_row, n_col, factor, plan),
        out_shape=(
            pltpu.VMEM((rows, width), jnp.float32),
            pltpu.VMEM((head_rows, head_cols), jnp.float32),
        ),
        in_specs=[pl.BlockSpec(memory_space=pl.ANY)] * 6,
        out_specs=(vmem, vmem),
        scratch_shapes=[
            pltpu.VMEM(pooled.shape, bf16),
            pltpu.VMEM(text_embed.shape, bf16),
            pltpu.VMEM(head_weight.shape, bf16),
            pltpu.SMEM(logit_scale.shape, f32),
            pltpu.SMEM(logit_bias.shape, f32),
            pltpu.VMEM(partner.shape, jnp.int32),
            dma((6,)),
            pltpu.VMEM((rows, width), f32),
            pltpu.VMEM((rows, width), bf16),
            pltpu.VMEM((rows, width), bf16),
            pltpu.VMEM((rows, width), bf16),
            pltpu.VMEM((n_row // 2, 2, head_rows, rows), bf16),
            pltpu.VMEM((8, 2, head_rows, rows), bf16),
            pltpu.VMEM((rows, width), bf16),
            pltpu.VMEM((rows, masked_width), bf16),
            pltpu.VMEM((n_col, image_rows, LANES), bf16),
            pltpu.VMEM((2, 8, image_rows, LANES), bf16),
            pltpu.VMEM((2, 2, out_rows, LANES), f32),
            pltpu.VMEM((2, out_rows, LANES), bf16),
            pltpu.VMEM((2, out_rows, LANES), bf16),
            pltpu.VMEM((out_rows, LANES), bf16),
            pltpu.VMEM((out_rows, LANES), bf16),
            dma((2,)),
            dma((2,)),
            dma((8,)),
            dma((8,)),
            dma((8, 2)),
            dma((8, 2)),
            dma((2, parts)),
            dma((2, parts)),
            dma((parts,)),
            dma((parts,)),
        ],
        compiler_params=pltpu.CompilerParams(collective_id=0, has_side_effects=True),
    )(pooled, text_embed, head_weight, logit_scale, logit_bias, partner)


def per_device(n_row, n_col):
    def run(pooled, text_embed, head_weight, logit_scale, logit_bias, partner):
        rows, width = pooled.shape
        fused = (
            n_row == 2**3
            and n_col == 2**2
            and rows == LANES
            and width % LANES == 0
            and width % (16 * n_row) == 0
            and width % n_col == 0
            and plan_of(rows, width, n_row, n_col) is not None
        )
        args = (pooled, text_embed, head_weight, logit_scale, logit_bias, partner)
        return deliver(*fused_body(n_row, n_col, *args)) if fused else body(*args)

    return run


def solution(mesh):
    in_specs = (
        P(("row", "col"), None),
        P(("row", "col"), None),
        P(),
        P(),
        P(),
        P(("row", "col"), None),
    )
    out_specs = (P(("row", "col"), None), P("row", "col"))
    run = per_device(mesh.shape["row"], mesh.shape["col"])
    return jax.shard_map(run, mesh=mesh, in_specs=in_specs, out_specs=out_specs, check_vma=False)
```

time: 33.6 us -> 32.4 us (0.964)
  Pallas kernels: 32.8 us -> 31.6 us
    pallas_call x1, Pallas kernels: 31.9 us -> 30.7 us  [fused_body(): pl.pallas_call(functools.partial(kernel, n_row, n_col, factor, plan), out...]
where the time goes in v2:
time: 32.4 us; the launch traced here: 32.3 us
  Pallas kernels  31.6 us (98%)
  between operations  0.64 us (2%)
    pallas_call x1, Pallas kernels, fused_body(): pl.pallas_call(functools.partial(kernel, n_row, n_col, factor, plan), out...  30.7 us
    pallas_call x1, Pallas kernels, deliver(): pl.pallas_call(move, out_shape=(jax.ShapeDtypeStruct(text_grad.shape, tex...  0.9 us

profile of v2, /device:TPU:0, one launch (start us, length us, event | category | flops | bytes accessed | tf_op | source)
XLA Modules:
  0.0 32.3 jit_solution(2616175862452384595)
XLA Ops:
  0.6 30.7 %shard_map.77 = (f32[128,1152]{1,0:T(8,128)S(1)}, f32[144,288]{1,0:T(8,128)S(1)}) custom-call(bf16[128,1152]{1,0:T(8,128)(2,1)} %pooled_hbm.1, bf16[128,1152]{1,0:T(8,128)(2,1)} %text_hbm.1, bf16[1152,1152]{1,0:T(8,128)(2,1)} %weight_hbm.1, f32[4]{0:T(128)} %scale_hbm.1, f32[4]{0:T(128)} %bias_hbm.1, s32[1,128]{1,0:T(1,128)} %partner_hbm.1), custom_call_target="tpu_custom_call" | custom-call | tf_op jit(solution)/shard_map/pallas_call | solution.py:629
  31.4 0.9 %shard_map.78 = (f32[128,1152]{1,0:T(8,128)}, f32[144,288]{1,0:T(8,128)}) custom-call(f32[128,1152]{1,0:T(8,128)S(1)} %get-tuple-element.4.text_from, f32[144,288]{1,0:T(8,128)S(1)} %get-tuple-element.5.head_from), custom_call_target="tpu_custom_call" | custom-call | tf_op jit(solution)/shard_map/pallas_call | solution.py:580

commit v3 on v2

--- a/solution.py
+++ b/solution.py
@@ -229,6 +229,7 @@
         (over_y_other, col),
         (row, over_z),
         (other_core, over_z),
+        (over_y, over_z),
         (row, far_z),
     )
     for peer in peers:
@@ -386,7 +387,7 @@
         image_copies[4, turn] = image_copy(theirs, 4, turn, (row, over_z))
         image_copies[2, turn] = image_copy(mine, 2, turn, (over_y, col))
         image_copies[1, turn] = image_copy(mine, 1, turn, (other_core, col))
-        image_copies[6, turn] = image_copy(held[4], 6, turn, (over_y, col))
+        image_copies[6, turn] = image_copy(theirs, 6, turn, (over_y, over_z))
         for slot in (3, 5, 7):
             image_copies[slot, turn] = image_copy(held[slot - 1], slot, turn, (other_core, col))
 
@@ -408,12 +409,11 @@
             image_sum[:, lanes] = image_sum[:, lanes] + value
 
         by_tile(image_piece, bounds, add_image)
-        for block in range(n_col):
+        def pack(block):
             first = block * head_cols // LANES * LANES
             offset = block * head_cols - first
-            part = image_sum[:, pl.ds(first, window)]
-            if offset:
-                part = pltpu.roll(part, window - offset, 1)
+            part = image_sum[:, pl.ds(pl.multiple_of(first, LANES), window)]
+            part = pltpu.roll(part, (window - offset) % window, 1)
             for n in range(tiles):
                 image_out[block, pl.ds(n * rows, rows), :] = part[
                     :, n * LANES : (n + 1) * LANES
@@ -421,9 +421,13 @@
             if tail:
                 last = folded(part[:, tiles * LANES : (tiles + 1) * LANES], image_tail)
                 image_out[block, pl.ds(tiles * rows, image_tail), :] = last.astype(jnp.bfloat16)
+
         for turn in range(2):
-            for slot in (4, 2, 1):
-                image_copies[slot, turn].start()
+            for slot in (4, 2):
+                pack(block_of(turn, 1 - pair if slot == 4 else pair))
+                if turn == 0:
+                    image_copies[slot + 2 if slot == 4 else 1, turn].start()
+                    image_copies[slot, turn].start()
 
         def own_text_piece(q, start, stop):
             return dot_nn(own[q].T, embed[:, pl.ds(start, stop - start)])
@@ -438,27 +442,28 @@
             cross_text[:, pl.ds(base, LANES)] = value.astype(jnp.bfloat16)
 
         by_tile(cross_text_piece, bounds, store_cross)
-        back_copy.start()
+
+        @pl.when(core + x > 0)
+        def _():
+            back_copy.start()
+
         by_tile(own_text_piece, bounds, store_text)
 
-    pl.when(core == 1)(cross_phase)
+    cross_phase()
     for slot in (6, 7):
         pool_copies[slot - 4].wait_recv()
         pool_copies[slot].start()
-    pl.when(core == 0)(cross_phase)
-
+
+    def forward(slot, turn):
+        image_copies[slot, turn].wait_recv()
+        image_copies[slot + 1, turn].start()
+
+    forward(4, 0)
+    forward(2, 0)
+    for slot in (6, 4, 2, 1):
+        image_copies[slot, 1].start()
     for turn in range(2):
         image_in[turn, 0] = image_out[block_of(turn, pair)]
-
-    def forward(slot, turn):
-        image_copies[slot, turn].wait_recv()
-        if slot == 4:
-            image_copies[6, turn].start()
-        image_copies[slot + 1, turn].start()
-
-    for turn in range(2):
-        forward(4, turn)
-        forward(2, turn)
     forward(6, 0)
     for slot in (1, 4, 5, 6, 7):
         pool_copies[slot].wait_recv()
@@ -521,17 +526,14 @@
                     pieces.append(moved.astype(jnp.bfloat16))
             keep_part(turn, tiles, dot_nn(left, jnp.concatenate(pieces, 0)))
 
-    @pl.when(core == 1)
+    multiply(0)
+
+    @pl.when(core + x == 0)
     def _():
-        forward(6, 1)
-
-    multiply(0)
-
-    @pl.when(core == 0)
-    def _():
-        forward(6, 1)
-
-    multiply(1)
+        back_copy.start()
+
+    for slot in (4, 2, 6):
+        forward(slot, 1)
     for n, (first, count) in enumerate(parts):
         at = pl.ds(first, count)
         x_copies[0, n].wait_recv()
@@ -539,6 +541,7 @@
         z_out[at, :] = value.astype(jnp.bfloat16)
         z_copies[n].start()
 
+    multiply(1)
     back_copy.wait_recv()
     text_grad_ref[...] = text_grad_ref[...] + text_back[...].astype(jnp.float32)
 

time: 32.4 us -> 29.8 us (0.920)
  Pallas kernels: 31.6 us -> 29 us
    pallas_call x1, Pallas kernels: 30.7 us -> 28.1 us  [fused_body(): pl.pallas_call(functools.partial(kernel, n_row, n_col, factor, plan), out...]
where the time goes in v3:
time: 29.8 us; the launch traced here: 29.7 us
  Pallas kernels  29 us (97%)
  between operations  0.64 us (2%)
    pallas_call x1, Pallas kernels, fused_body(): pl.pallas_call(functools.partial(kernel, n_row, n_col, factor, plan), out...  28.1 us
    pallas_call x1, Pallas kernels, deliver(): pl.pallas_call(move, out_shape=(jax.ShapeDtypeStruct(text_grad.shape, tex...  0.9 us

profile of v3, /device:TPU:0, one launch (start us, length us, event | category | flops | bytes accessed | tf_op | source)
XLA Modules:
  0.0 29.7 jit_solution(14770019695209641940)
XLA Ops:
  0.6 28.1 %shard_map.77 = (f32[128,1152]{1,0:T(8,128)S(1)}, f32[144,288]{1,0:T(8,128)S(1)}) custom-call(bf16[128,1152]{1,0:T(8,128)(2,1)} %pooled_hbm.1, bf16[128,1152]{1,0:T(8,128)(2,1)} %text_hbm.1, bf16[1152,1152]{1,0:T(8,128)(2,1)} %weight_hbm.1, f32[4]{0:T(128)} %scale_hbm.1, f32[4]{0:T(128)} %bias_hbm.1, s32[1,128]{1,0:T(1,128)} %partner_hbm.1), custom_call_target="tpu_custom_call" | custom-call | tf_op jit(solution)/shard_map/pallas_call | solution.py:632
  28.8 0.9 %shard_map.78 = (f32[128,1152]{1,0:T(8,128)}, f32[144,288]{1,0:T(8,128)}) custom-call(f32[128,1152]{1,0:T(8,128)S(1)} %get-tuple-element.4.text_from, f32[144,288]{1,0:T(8,128)S(1)} %get-tuple-element.5.head_from), custom_call_target="tpu_custom_call" | custom-call | tf_op jit(solution)/shard_map/pallas_call | solution.py:583

commit v4 on v3

--- a/solution.py
+++ b/solution.py
@@ -287,7 +287,8 @@
             at = stop
 
     def pool_copy(src, slot, device):
-        return remote(src, pooled_in.at[slot], pool_send.at[slot], pool_recv.at[slot], device)
+        wait = {2: 1, 3: 2}.get(slot, 0)
+        return remote(src, pooled_in.at[slot], pool_send, pool_recv.at[wait], device)
 
     def pooled_for(half_y, half_core):
         return pooled_t.at[pl.ds(2 * half_y, 2), half_core]
@@ -374,8 +375,8 @@
         return remote(
             src,
             image_in.at[turn, slot],
-            image_send.at[slot, turn],
-            image_recv.at[slot, turn],
+            image_send,
+            image_recv.at[slot // 2 if slot % 2 == 0 else 0, turn],
             device,
         )
 
@@ -458,15 +459,20 @@
         image_copies[slot, turn].wait_recv()
         image_copies[slot + 1, turn].start()
 
+    for slot in (6, 4, 2, 1):
+        image_copies[slot, 1].start()
+
+    def forward_second():
+        for slot in (4, 2, 6):
+            forward(slot, 1)
+
     forward(4, 0)
     forward(2, 0)
-    for slot in (6, 4, 2, 1):
-        image_copies[slot, 1].start()
     for turn in range(2):
         image_in[turn, 0] = image_out[block_of(turn, pair)]
     forward(6, 0)
-    for slot in (1, 4, 5, 6, 7):
-        pool_copies[slot].wait_recv()
+    several = pooled_in.at[pl.ds(0, 5)]
+    remote(several, several, pool_send, pool_recv.at[0], (other_core, col)).wait_recv()
 
     parts = [(n * head_rows, head_rows) for n in range(tiles)]
     if tail:
@@ -479,15 +485,15 @@
         (turn, n): remote(
             part_of(x_out.at[turn], n),
             part_of(x_in.at[turn], n),
-            x_send.at[turn, n],
-            x_recv.at[turn, n],
+            x_send,
+            x_recv.at[n if turn == 0 else len(parts)],
             (over_x, col),
         )
         for turn in range(2)
         for n in range(len(parts))
     }
     z_copies = [
-        remote(part_of(z_out, n), part_of(z_in, n), z_send.at[n], z_recv.at[n], (row, far_z))
+        remote(part_of(z_out, n), part_of(z_in, n), z_send, z_recv, (row, far_z))
         for n in range(len(parts))
     ]
 
@@ -504,8 +510,10 @@
         x_copies[turn, n].start()
 
     def multiply(turn):
-        for slot in (1, 3, 5, 7):
-            image_copies[slot, turn].wait_recv()
+        several = image_in.at[turn, pl.ds(0, 4)]
+        remote(
+            several, several, image_send, image_recv.at[0, turn], (other_core, col)
+        ).wait_recv()
         left = jnp.concatenate(
             [pooled_in[slot].reshape(2 * head_rows, rows) for slot in range(8)], 1
         )
@@ -532,8 +540,7 @@
     def _():
         back_copy.start()
 
-    for slot in (4, 2, 6):
-        forward(slot, 1)
+    forward_second()
     for n, (first, count) in enumerate(parts):
         at = pl.ds(first, count)
         x_copies[0, n].wait_recv()
@@ -545,11 +552,12 @@
     back_copy.wait_recv()
     text_grad_ref[...] = text_grad_ref[...] + text_back[...].astype(jnp.float32)
 
+    all_z = remote(z_out, z_in, z_send, z_recv, (row, far_z))
+    remote(x_out.at[1], x_in.at[1], x_send, x_recv.at[len(parts)], (over_x, col)).wait_recv()
+    all_z.wait_recv()
     for n, (first, count) in enumerate(parts):
         at = pl.ds(first, count)
-        x_copies[1, n].wait_recv()
         value = total[1, x, at, :] + x_in[1, at, :].astype(jnp.float32)
-        z_copies[n].wait_recv()
         value = value + z_in[at, :].astype(jnp.float32)
         if n < tiles:
             head_grad_ref[:, pl.ds(n * LANES, LANES)] = value
@@ -560,11 +568,12 @@
 
     behind_copy.wait_send()
     back_copy.wait_send()
-    for copies in (pool_copies, image_copies, x_copies):
-        for name in sorted(copies):
-            copies[name].wait_send()
-    for copy in z_copies:
-        copy.wait_send()
+    several = pooled_in.at[pl.ds(0, 7)]
+    remote(several, several, pool_send, pool_recv.at[0], (other_core, col)).wait_send()
+    several = image_in.at[:, pl.ds(0, 7)]
+    remote(several, several, image_send, image_recv.at[0, 0], (other_core, col)).wait_send()
+    remote(x_out, x_in, x_send, x_recv.at[0], (over_x, col)).wait_send()
+    all_z.wait_send()
 
 
 def deliver(text_grad, head_grad):
@@ -662,14 +671,14 @@
             pltpu.VMEM((out_rows, LANES), bf16),
             dma((2,)),
             dma((2,)),
-            dma((8,)),
-            dma((8,)),
-            dma((8, 2)),
-            dma((8, 2)),
-            dma((2, parts)),
-            dma((2, parts)),
-            dma((parts,)),
-            dma((parts,)),
+            dma,
+            dma((3,)),
+            dma,
+            dma((4, 2)),
+            dma,
+            dma((parts + 1,)),
+            dma,
+            dma,
         ],
         compiler_params=pltpu.CompilerParams(collective_id=0, has_side_effects=True),
     )(pooled, text_embed, head_weight, logit_scale, logit_bias, partner)

time: 29.8 us -> 29.4 us (0.987)
  Pallas kernels: 29 us -> 28.6 us
    pallas_call x1, Pallas kernels: 28.1 us -> 27.7 us  [fused_body(): pl.pallas_call(functools.partial(kernel, n_row, n_col, factor, plan), out...]
where the time goes in v4:
time: 29.4 us; the launch traced here: 29.2 us
  Pallas kernels  28.6 us (97%)
  between operations  0.64 us (2%)
    pallas_call x1, Pallas kernels, fused_body(): pl.pallas_call(functools.partial(kernel, n_row, n_col, factor, plan), out...  27.7 us
    pallas_call x1, Pallas kernels, deliver(): pl.pallas_call(move, out_shape=(jax.ShapeDtypeStruct(text_grad.shape, tex...  0.9 us

profile of v4, /device:TPU:0, one launch (start us, length us, event | category | flops | bytes accessed | tf_op | source)
XLA Modules:
  0.0 29.2 jit_solution(3369398024699823080)
XLA Ops:
  0.6 27.7 %shard_map.77 = (f32[128,1152]{1,0:T(8,128)S(1)}, f32[144,288]{1,0:T(8,128)S(1)}) custom-call(bf16[128,1152]{1,0:T(8,128)(2,1)} %pooled_hbm.1, bf16[128,1152]{1,0:T(8,128)(2,1)} %text_hbm.1, bf16[1152,1152]{1,0:T(8,128)(2,1)} %weight_hbm.1, f32[4]{0:T(128)} %scale_hbm.1, f32[4]{0:T(128)} %bias_hbm.1, s32[1,128]{1,0:T(1,128)} %partner_hbm.1), custom_call_target="tpu_custom_call" | custom-call | tf_op jit(solution)/shard_map/pallas_call | solution.py:641
  28.3 0.9 %shard_map.78 = (f32[128,1152]{1,0:T(8,128)}, f32[144,288]{1,0:T(8,128)}) custom-call(f32[128,1152]{1,0:T(8,128)S(1)} %get-tuple-element.4.text_from, f32[144,288]{1,0:T(8,128)S(1)} %get-tuple-element.5.head_from), custom_call_target="tpu_custom_call" | custom-call | tf_op jit(solution)/shard_map/pallas_call | solution.py:592
